TPU v7x, 256 devices: a whole 4x4x8 slice. The times are simulated.
256 devices in a mesh: tm: 32 (over z, x), region: 8 (over y, core).
Axes of the slice: x: 4, y: 4, z: 8, core: 2. Of those that a mesh axis runs over, the one named last changes fastest.
Arguments:
- start_primal: float32 [2048, 8, 3200], P('tm', 'region'), may hold values from 0 to 10, as said below
- demand: float32 [2048, 8, 3200], P('tm', 'region'), may hold values from -30 to 30
- unit_cost: float32 [8, 3200], P('region'), may hold values from -5 to 5
- build_cost: float32 [8, 128], P('region', 'tm'), may hold values from 0.5 to 2
- start_capacity: float32 [8, 128], P('region', 'tm'), may hold values from 0 to 2
- net_weights: float32 [8, 25, 3, 128, 128], P('region'), may hold values from -0.3125 to 0.3125
- net_columns: int32 [8, 25, 3], P('region'), may hold values from 0 to 24
- line_weights: float32 [8, 4, 128, 128], P('region'), may hold values from -0.25 to 0.25
- line_source: int32 [8, 4], replicated, may hold values from 0 to 7
- generator_map: int32 [8, 128], P('region'), may hold values from 0 to 127
Outputs:
- primal_final: float32 [2048, 8, 3200], P('tm', 'region')
- dual_final: float32 [2048, 8, 3200], P('tm', 'region')
- capacity_final: float32 [8, 128], P('region', 'tm')
Inputs may be any that keep to these rules, and one draw needn't show every extreme that they name: `start_primal`: Nonnegative.
All inputs are finite; a program needn't handle non-finite values.
Results may differ from a plain program's by a relative error of at most 0.0003.
Values sent between devices are 32-bit elements; how exact they have to be, the bound alone decides.
A program may use at most 64 MiB of HBM per device.

v0:
```python
import math
import jax
import jax.numpy as jnp
from jax import lax
from jax.sharding import PartitionSpec as P

ITERS = 4
HIGHEST_PRECISION = lax.Precision.HIGHEST
STEP_SCALE = 0.2
EPSILON = 1e-06


def shifted(shard, axis, by):
    devices = lax.axis_size(axis)
    pairs = [(i, i + by) for i in range(devices) if 0 <= i + by < devices]
    return lax.ppermute(shard, axis, pairs)


def network_forward(blocks, weights, columns):
    hour_count = blocks.shape[0]
    picked = jnp.take(blocks, columns.reshape(-1), axis=1)
    flat_weights = weights.reshape(-1, weights.shape[2], weights.shape[3])
    product = jnp.einsum("hpk,pkl->hpl", picked, flat_weights, precision=HIGHEST_PRECISION)
    return product.reshape(hour_count, columns.shape[0], columns.shape[1], -1).sum(axis=2)


def network_adjoint(dual_rows, weights, columns):
    hour_count = dual_rows.shape[0]
    partial_value = jnp.einsum("hil,iskl->hisk", dual_rows, weights, precision=HIGHEST_PRECISION)
    block_count = columns.shape[0]
    placing = (columns.reshape(-1)[:, None] == jnp.arange(block_count)[None, :]).astype(jnp.float32)
    stacked = partial_value.reshape(hour_count, -1, partial_value.shape[3])
    return jnp.einsum("hpk,pc->hck", stacked, placing, precision=HIGHEST_PRECISION)


def body(
    start_primal,
    demand,
    unit_cost,
    build_cost,
    start_capacity,
    net_weights,
    net_columns,
    line_weights,
    line_source,
    generator_map,
):
    hour_count, _, row_width = start_primal.shape
    block_size = net_weights.shape[3]
    block_count = row_width // block_size
    tm_count = lax.axis_size("tm")
    region_count = lax.axis_size("region")
    own_region = lax.axis_index("region")
    weights = net_weights[0]
    columns = net_columns[0]
    line_mats = line_weights[0]
    unit_rows = unit_cost.reshape(block_count, block_size)
    invest_own = start_capacity.shape[1]
    invest_all = invest_own * tm_count
    couple = 1.0 / math.sqrt(hour_count * tm_count)
    primal_count = hour_count * tm_count * region_count * row_width + region_count * invest_all
    dual_count = hour_count * tm_count * region_count * row_width
    selector = (generator_map[0][:, None] == jnp.arange(invest_all)[None, :]).astype(jnp.float32)
    line_links = (line_source[:, :, None] == jnp.arange(region_count)[None, None, :]).astype(
        jnp.float32
    )
    own_sources = lax.dynamic_index_in_dim(line_links, own_region, 0, keepdims=False)
    free_column = (jnp.arange(block_count) == 3)[None, :, None]
    free_row = (jnp.arange(block_count) < 3)[None, :, None]
    primal = start_primal.reshape(hour_count, block_count, block_size)
    target = demand.reshape(hour_count, block_count, block_size)
    dual = jnp.zeros_like(primal)
    primal_weight = jnp.float32(1.0)
    capacity, build_rows = (
        lax.all_gather(start_capacity[0], "tm", axis=0, tiled=True),
        lax.all_gather(build_cost[0], "tm", axis=0, tiled=True),
    )
    for iteration in range(ITERS):
        primal_step = STEP_SCALE / primal_weight
        dual_step = STEP_SCALE * primal_weight
        adjoint = network_adjoint(dual, weights, columns)
        after = shifted(dual[0, 0], "tm", -1)
        following = jnp.concatenate([dual[1:, 0], after[None]], axis=0)
        partial_lines = jnp.einsum(
            "hl,jkl->jhk", dual[:, 1], line_mats, precision=HIGHEST_PRECISION
        )
        line_back = lax.psum_scatter(
            jnp.einsum("jq,jhk->qhk", own_sources, partial_lines, precision=HIGHEST_PRECISION),
            "region",
            scatter_dimension=0,
            tiled=True,
        )[0]
        adjoint = adjoint.at[:, 0].add(-following).at[:, 3].add(line_back)
        column_sums = jnp.sum(dual[:, 2], axis=0)
        capacity_part = couple * jnp.dot(column_sums, selector, precision=HIGHEST_PRECISION)
        moved = primal - primal_step * (unit_rows[None] - adjoint)
        new_primal = jnp.where(free_column, moved, jnp.maximum(moved, 0.0))
        capacity_grad = lax.psum(capacity_part, "tm")
        new_capacity = jnp.maximum(capacity - primal_step * (build_rows - capacity_grad), 0.0)
        capacity_bar = 2.0 * new_capacity - capacity
        capacity_change = lax.dynamic_slice_in_dim(
            new_capacity - capacity, lax.axis_index("tm") * invest_own, invest_own, 0
        )
        primal_bar = 2.0 * new_primal - primal
        primal_local = jnp.sum((new_primal - primal) ** 2) + jnp.sum(capacity_change**2)
        if iteration + 1 < ITERS:
            primal_total = lax.psum(primal_local, ("tm", "region"))
        applied = network_forward(primal_bar, weights, columns)
        before = shifted(primal_bar[-1, 0], "tm", 1)
        earlier = jnp.concatenate([before[None], primal_bar[:-1, 0]], axis=0)
        chosen_flows = jnp.einsum(
            "jr,rhk->jhk",
            own_sources,
            lax.all_gather(primal_bar[:, 3][None], "region", axis=0, tiled=True),
            precision=HIGHEST_PRECISION,
        )
        line_flow = jnp.einsum("jhk,jkl->hl", chosen_flows, line_mats, precision=HIGHEST_PRECISION)
        picked_capacity = jnp.dot(selector, capacity_bar, precision=HIGHEST_PRECISION)
        applied = (
            applied.at[:, 0]
            .add(-earlier)
            .at[:, 1]
            .add(line_flow)
            .at[:, 2]
            .add(couple * picked_capacity[None])
        )
        moved_dual = dual + dual_step * (target - applied)
        new_dual = jnp.where(free_row, moved_dual, jnp.maximum(moved_dual, 0.0))
        if iteration + 1 < ITERS:
            dual_local = jnp.sum((new_dual - dual) ** 2)
            dual_total = lax.psum(dual_local, ("tm", "region"))
            primal_weight = jnp.sqrt(
                primal_weight
                * jnp.sqrt(primal_total / primal_count + EPSILON)
                / jnp.sqrt(dual_total / dual_count + EPSILON)
            )
        primal, dual, capacity = (new_primal, new_dual, new_capacity)
    capacity_own = lax.dynamic_slice_in_dim(
        capacity, lax.axis_index("tm") * invest_own, invest_own, 0
    )
    return (
        primal.reshape(hour_count, 1, row_width),
        dual.reshape(hour_count, 1, row_width),
        capacity_own[None],
    )


def solution(mesh):
    in_specs = (
        P("tm", "region", None),
        P("tm", "region", None),
        P("region", None),
        P("region", "tm"),
        P("region", "tm"),
        P("region", None, None, None, None),
        P("region", None, None),
        P("region", None, None, None),
        P(),
        P("region", None),
    )
    out_specs = (P("tm", "region", None), P("tm", "region", None), P("region", "tm"))
    return jax.shard_map(body, mesh=mesh, in_specs=in_specs, out_specs=out_specs, check_vma=False)
```

profile of v0, /device:TPU:1, one launch (start us, length us, event | category | flops | bytes accessed | tf_op | source)
XLA Modules:
  0.0 858.2 jit_solution(13189949462657411320)
XLA Ops:
  12.9 9.0 %fusion.6 = f32[25,64,3,128]{3,1,2,0:T(8,128)S(1)} fusion(f32[1,25,3,128,128]{4,3,2,1,0:T(8,128)} %param.57), kind=kOutput, calls=%fused_computation.10 | convolution fusion | flops 943718400 | bytes 7372800 | tf_op jit(solution)/shard_map/hil,iskl->hisk/dot_general | solution.py:29
  27.1 76.9 %all-reduce.6 = (f32[128]{0:T(128)S(1)}, f32[128]{0:T(128)S(1)}, f32[128]{0:T(128)S(1)}) all-reduce(f32[128]{0:T(128)S(1)} %bitcast_dynamic-update-slice_fusion.1, f32[128]{0:T(128)S(1)} %bitcast_dynamic-update-slice_fusion, f32[128]{0:T(128)S(1)} %fusion.51), channel_id=2, replica_groups=mesh['tm'=32,'region'=8] {'tm'}, use_global_device_ids=true, to_apply=%add.1 | all-reduce | flops 384 | bytes 3072 | tf_op jit(solution)/shard_map/all_gather | solution.py:75
  113.3 28.2 %all-gather.2 = f32[512,1,128]{2,1,0:T(1,128)S(1)} all-gather(f32[64,1,128]{2,1,0:T(1,128)S(1)} %bitcast.385), channel_id=4, replica_groups=mesh['tm'=32,'region'=8] {'region'}, dimensions={0}, use_global_device_ids=true | all-gather | bytes 294912 | tf_op jit(solution)/shard_map/all_gather | solution.py:114
  143.6 7.9 fusion.22
  157.0 10.5 %fusion.4 = f32[25,64,3,128]{3,1,2,0:T(8,128)} fusion(f32[1,25,3,128,128]{4,3,2,1,0:T(8,128)} %param.57, f32[64,25,128]{2,0,1:T(8,128)S(1)} %get-tuple-element.281), kind=kOutput, calls=%fused_computation.8 | convolution fusion | flops 943718400 | bytes 8192000 | tf_op jit(solution)/shard_map/hil,iskl->hisk/dot_general | solution.py:29
  167.7 55.8 %psum.73 = f32[128]{0:T(128)S(1)} all-reduce(f32[128]{0:T(128)S(1)} %fusion.49), channel_id=1, replica_groups=mesh['tm'=32,'region'=8] {'tm'}, use_global_device_ids=true, to_apply=%region_11.13 | all-reduce | flops 128 | bytes 1024 | tf_op jit(solution)/shard_map/psum | solution.py:98
  223.5 89.7 %all-reduce.5 = (f32[]{:T(128)}, f32[]{:T(128)}) all-reduce(f32[]{:T(128)S(6)} %add.249, f32[]{:T(128)} %get-tuple-element.280), channel_id=1, replica_groups=mesh['tm'=32,'region'=8] {'tm','region'}, use_global_device_ids=true, to_apply=%region_4.5 | all-reduce | flops 2 | bytes 16 | tf_op jit(solution)/shard_map/psum | solution.py:107
  317.6 4.0 fusion.12
  325.8 22.6 %reduce-scatter.7.cloned.1.call-done = f32[1,64,128]{2,1,0:T(8,128)} async-done(((f32[8,64,128]{2,1,0:T(8,128)}), f32[1,64,128]{2,1,0:T(8,128)}) %reduce-scatter.7.cloned.1.call-update) | async-done | bytes 32784 | tf_op jit(solution)/shard_map/reduce_scatter | solution.py:87
  357.8 16.1 %all-gather.3 = f32[512,1,128]{2,1,0:T(1,128)S(1)} all-gather(f32[64,1,128]{2,1,0:T(1,128)S(1)} %bitcast.383), channel_id=5, replica_groups=mesh['tm'=32,'region'=8] {'region'}, dimensions={0}, use_global_device_ids=true | all-gather | bytes 294912 | tf_op jit(solution)/shard_map/all_gather | solution.py:114
  373.9 7.9 fusion.20
  387.2 10.5 %fusion.2 = f32[25,64,3,128]{3,1,2,0:T(8,128)} fusion(f32[1,25,3,128,128]{4,3,2,1,0:T(8,128)} %param.57, f32[64,25,128]{2,0,1:T(8,128)S(1)} %get-tuple-element.275), kind=kOutput, calls=%fused_computation.6 | convolution fusion | flops 943718400 | bytes 8192000 | tf_op jit(solution)/shard_map/hil,iskl->hisk/dot_general | solution.py:29
  397.9 59.1 %psum.76 = f32[128]{0:T(128)S(1)} all-reduce(f32[128]{0:T(128)S(1)} %fusion.47), channel_id=1, replica_groups=mesh['tm'=32,'region'=8] {'tm'}, use_global_device_ids=true, to_apply=%region_20.22 | all-reduce | flops 128 | bytes 1024 | tf_op jit(solution)/shard_map/psum | solution.py:98
  457.0 86.0 %all-reduce.4 = (f32[]{:T(128)}, f32[]{:T(128)}) all-reduce(f32[]{:T(128)S(6)} %add.257, f32[]{:T(128)} %get-tuple-element.274), channel_id=1, replica_groups=mesh['tm'=32,'region'=8] {'tm','region'}, use_global_device_ids=true, to_apply=%region_13.15 | all-reduce | flops 2 | bytes 16 | tf_op jit(solution)/shard_map/psum | solution.py:107
  547.2 4.0 fusion.10
  555.4 23.9 %reduce-scatter.9.cloned.1.call-done = f32[1,64,128]{2,1,0:T(8,128)} async-done(((f32[8,64,128]{2,1,0:T(8,128)}), f32[1,64,128]{2,1,0:T(8,128)}) %reduce-scatter.9.cloned.1.call-update) | async-done | bytes 32784 | tf_op jit(solution)/shard_map/reduce_scatter | solution.py:87
  587.9 16.1 %all-gather.4 = f32[512,1,128]{2,1,0:T(1,128)S(1)} all-gather(f32[64,1,128]{2,1,0:T(1,128)S(1)} %bitcast.384), channel_id=6, replica_groups=mesh['tm'=32,'region'=8] {'region'}, dimensions={0}, use_global_device_ids=true | all-gather | bytes 294912 | tf_op jit(solution)/shard_map/all_gather | solution.py:114
  604.0 7.9 fusion.18
  618.5 10.5 %fusion = f32[25,64,3,128]{3,1,2,0:T(8,128)} fusion(f32[1,25,3,128,128]{4,3,2,1,0:T(8,128)} %param.57, f32[64,25,128]{2,0,1:T(8,128)S(1)} %get-tuple-element.271), kind=kOutput, calls=%fused_computation.4 | convolution fusion | flops 943718400 | bytes 8192000 | tf_op jit(solution)/shard_map/hil,iskl->hisk/dot_general | solution.py:29
  629.2 59.1 %psum.79 = f32[128]{0:T(128)S(1)} all-reduce(f32[128]{0:T(128)S(1)} %fusion.45), channel_id=1, replica_groups=mesh['tm'=32,'region'=8] {'tm'}, use_global_device_ids=true, to_apply=%region_29.31 | all-reduce | flops 128 | bytes 1024 | tf_op jit(solution)/shard_map/psum | solution.py:98
  688.3 86.0 %all-reduce.3 = (f32[]{:T(128)}, f32[]{:T(128)}) all-reduce(f32[]{:T(128)S(6)} %add.266, f32[]{:T(128)} %get-tuple-element.270), channel_id=1, replica_groups=mesh['tm'=32,'region'=8] {'tm','region'}, use_global_device_ids=true, to_apply=%region_22.24 | all-reduce | flops 2 | bytes 16 | tf_op jit(solution)/shard_map/psum | solution.py:107
  786.6 24.2 %reduce-scatter.11.cloned.1.call-done = f32[1,64,128]{2,1,0:T(8,128)} async-done(((f32[8,64,128]{2,1,0:T(8,128)}), f32[1,64,128]{2,1,0:T(8,128)}) %reduce-scatter.11.cloned.1.call-update) | async-done | bytes 32784 | tf_op jit(solution)/shard_map/reduce_scatter | solution.py:87
  819.9 16.1 %all-gather.5 = f32[512,1,128]{2,1,0:T(1,128)S(1)} all-gather(f32[64,1,128]{2,1,0:T(1,128)S(1)} %bitcast.382), channel_id=7, replica_groups=mesh['tm'=32,'region'=8] {'region'}, dimensions={0}, use_global_device_ids=true | all-gather | bytes 294912 | tf_op jit(solution)/shard_map/all_gather | solution.py:114
  836.0 8.0 fusion.16
  (182 shorter events, 94.8 us)
Async XLA Ops:
  7.2 97.1 %copy-start = (f32[64,1,3200]{2,1,0:T(1,128)S(1)}, f32[64,1,3200]{2,1,0:T(1,128)}, u32[]{:S(2)}) copy-start(f32[64,1,3200]{2,1,0:T(1,128)} %param.53) | copy-start | bytes 2457604
  7.2 102.9 %reduce-scatter.5.cloned.1.call-start = ((), (), s32[]{:S(2)}) async-start(), calls=%async_computation.4 | async-start | bytes 294912 | tf_op jit(solution)/shard_map/reduce_scatter | solution.py:87
  7.2 102.8 %collective-permute-start = (f32[128]{0:T(128)S(1)}, f32[128]{0:T(128)S(1)}, u32[]{:S(2)}, u32[]{:S(2)}) collective-permute-start(f32[128]{0:T(128)S(1)} %broadcast.305), channel_id=1, source_target_pairs={{8,0},{16,8},{24,16},{32,24},{40,32},{48,40},{56,48},{64,56},{72,6... | collective-permute-start | bytes 1544 | tf_op jit(solution)/shard_map/ppermute | solution.py:16
  12.0 336.4 %reduce-scatter.7.cloned.1.call-start = ((), (), s32[]{:S(2)}) async-start(), calls=%async_computation.5 | async-start | bytes 294912 | tf_op jit(solution)/shard_map/reduce_scatter | solution.py:87
  24.4 2.6 copy-start.13
  24.4 79.8 %copy-start.11 = (f32[1,3200]{1,0:T(1,128)S(1)}, f32[1,3200]{1,0:T(1,128)}, u32[]{:S(2)}) copy-start(f32[1,3200]{1,0:T(1,128)} %param.54) | copy-start | bytes 38404
  112.0 43.3 %collective-permute-start.1 = (f32[128]{0:T(128)S(1)}, f32[128]{0:T(128)S(1)}, u32[]{:S(2)}, u32[]{:S(2)}) collective-permute-start(f32[128]{0:T(128)S(1)} %slice_bitcast_fusion.16), channel_id=1, source_target_pairs={{0,8},{8,16},{16,24},{24,32},{32,40},{40,48},{48,56},{56,64},{64,7... | collective-permute-start | bytes 1544 | tf_op jit(solution)/shard_map/ppermute | solution.py:16
  151.5 3.8 copy-start.2
  156.6 10.9 %copy-start.8 = (f32[64,25,128]{2,0,1:T(8,128)}, f32[64,25,128]{2,0,1:T(8,128)S(1)}, u32[]{:S(2)}) copy-start(f32[64,25,128]{2,0,1:T(8,128)S(1)} %get-tuple-element.281) | copy-start | bytes 2457604
  167.7 153.9 %copy-start.15 = (s32[1,128]{1,0:T(1,128)S(1)}, s32[1,128]{1,0:T(1,128)}, u32[]{:S(2)}) copy-start(s32[1,128]{1,0:T(1,128)} %param.61) | copy-start | bytes 1540
  314.6 10.5 %collective-permute-start.2 = (f32[128]{0:T(128)S(1)}, f32[128]{0:T(128)S(1)}, u32[]{:S(2)}, u32[]{:S(2)}) collective-permute-start(f32[128]{0:T(128)S(1)} %slice_bitcast_fusion.15), channel_id=1, source_target_pairs={{8,0},{16,8},{24,16},{32,24},{40,32},{48,40},{56,48},{64,56},{72,6... | collective-permute-start | bytes 1544 | tf_op jit(solution)/shard_map/ppermute | solution.py:16
  317.1 262.2 %reduce-scatter.9.cloned.1.call-start = ((), (), s32[]{:S(2)}) async-start(), calls=%async_computation.6 | async-start | bytes 294912 | tf_op jit(solution)/shard_map/reduce_scatter | solution.py:87
  354.9 30.4 %collective-permute-start.3 = (f32[128]{0:T(128)S(1)}, f32[128]{0:T(128)S(1)}, u32[]{:S(2)}, u32[]{:S(2)}) collective-permute-start(f32[128]{0:T(128)S(1)} %slice_bitcast_fusion.14), channel_id=1, source_target_pairs={{0,8},{8,16},{16,24},{24,32},{32,40},{40,48},{48,56},{56,64},{64,7... | collective-permute-start | bytes 1544 | tf_op jit(solution)/shard_map/ppermute | solution.py:16
  381.8 4.0 copy-start.9
  386.8 10.9 %copy-start.7 = (f32[64,25,128]{2,0,1:T(8,128)}, f32[64,25,128]{2,0,1:T(8,128)S(1)}, u32[]{:S(2)}) copy-start(f32[64,25,128]{2,0,1:T(8,128)S(1)} %get-tuple-element.275) | copy-start | bytes 2457604
  544.5 10.3 %collective-permute-start.4 = (f32[128]{0:T(128)S(1)}, f32[128]{0:T(128)S(1)}, u32[]{:S(2)}, u32[]{:S(2)}) collective-permute-start(f32[128]{0:T(128)S(1)} %slice_bitcast_fusion.13), channel_id=1, source_target_pairs={{8,0},{16,8},{24,16},{32,24},{40,32},{48,40},{56,48},{64,56},{72,6... | collective-permute-start | bytes 1544 | tf_op jit(solution)/shard_map/ppermute | solution.py:16
  547.0 263.9 %reduce-scatter.11.cloned.1.call-start = ((), (), s32[]{:S(2)}) async-start(), calls=%async_computation.7 | async-start | bytes 294912 | tf_op jit(solution)/shard_map/reduce_scatter | solution.py:87
  551.2 29.5 %copy-start.4 = (f32[64,25,128]{2,0,1:T(8,128)S(1)}, f32[64,25,128]{2,0,1:T(8,128)}, u32[]{:S(2)}) copy-start(f32[64,25,128]{2,0,1:T(8,128)} %copy-done.3) | copy-start | bytes 2457604
  585.1 30.5 %collective-permute-start.5 = (f32[128]{0:T(128)S(1)}, f32[128]{0:T(128)S(1)}, u32[]{:S(2)}, u32[]{:S(2)}) collective-permute-start(f32[128]{0:T(128)S(1)} %slice_bitcast_fusion.12), channel_id=1, source_target_pairs={{0,8},{8,16},{16,24},{24,32},{32,40},{40,48},{48,56},{56,64},{64,7... | collective-permute-start | bytes 1544 | tf_op jit(solution)/shard_map/ppermute | solution.py:16
  618.1 10.9 %copy-start.5 = (f32[64,25,128]{2,0,1:T(8,128)}, f32[64,25,128]{2,0,1:T(8,128)S(1)}, u32[]{:S(2)}) copy-start(f32[64,25,128]{2,0,1:T(8,128)S(1)} %get-tuple-element.271) | copy-start | bytes 2457604
  775.8 10.2 %collective-permute-start.6 = (f32[128]{0:T(128)S(1)}, f32[128]{0:T(128)S(1)}, u32[]{:S(2)}, u32[]{:S(2)}) collective-permute-start(f32[128]{0:T(128)S(1)} %slice_bitcast_fusion.11), channel_id=1, source_target_pairs={{8,0},{16,8},{24,16},{32,24},{40,32},{48,40},{56,48},{64,56},{72,6... | collective-permute-start | bytes 1544 | tf_op jit(solution)/shard_map/ppermute | solution.py:16
  817.0 31.6 %collective-permute-start.7 = (f32[128]{0:T(128)S(1)}, f32[128]{0:T(128)S(1)}, u32[]{:S(2)}, u32[]{:S(2)}) collective-permute-start(f32[128]{0:T(128)S(1)} %slice_bitcast_fusion.10), channel_id=1, source_target_pairs={{0,8},{8,16},{16,24},{24,32},{32,40},{40,48},{48,56},{56,64},{64,7... | collective-permute-start | bytes 1544 | tf_op jit(solution)/shard_map/ppermute | solution.py:16
  836.0 8.4 copy-start.10
  844.9 4.1 copy-start.6
  (5 other events, 8.1 us)
Sparse Core Ops, SparseCore 0:
  12.1 36.2 reduce-scatter.4
  317.2 31.0 reduce-scatter.6
  547.1 32.1 reduce-scatter.8
  778.6 32.1 reduce-scatter.10
where the time goes:
time: 867 us; the launch traced here: 858 us
  blocking collectives  589 us (68%)
  matrix products  94.9 us (11%)
  waiting for transfers between devices  70.8 us (8%)
  other arithmetic  35 us (4%)
  local copies, waits for them, and re-layouts  28.8 us (3%)
  between operations  23.7 us (3%)
  starting transfers between devices  16 us (2%)
    psum x3, blocking collectives, body(): primal_total = lax.psum(primal_local, ('tm', 'region'))  262 us
    psum x3, blocking collectives, body(): capacity_grad = lax.psum(capacity_part, 'tm')  174 us
    all_gather x1, blocking collectives, body(): lax.all_gather(start_capacity[0], 'tm', axis=0, tiled=True)  76.9 us
    all_gather x4, blocking collectives, body(): lax.all_gather(primal_bar[:, 3][None], 'region', axis=0, tiled=True)  76.5 us
    reduce_scatter x4, waiting for transfers between devices, body(): lax.psum_scatter(jnp.einsum('jq,jhk->qhk', own_sources, partial_lines, pr...  70.7 us
    dot_general x4, matrix products, network_adjoint(): jnp.einsum('hil,iskl->hisk', dual_rows, weights, precision=HIGHEST_PRECIS...  40.4 us
    dot_general x4, matrix products, network_forward(): jnp.einsum('hpk,pkl->hpl', picked, flat_weights, precision=HIGHEST_PRECIS...  31.7 us
  transfers between devices with their start and end apart: 12, of which 3 were waited for; matrix products, arithmetic and copies ran while one was open for 11% of the time, Pallas kernels for 0%

commit v1 on v0

--- a/solution.py
+++ b/solution.py
@@ -104,7 +104,7 @@
         primal_bar = 2.0 * new_primal - primal
         primal_local = jnp.sum((new_primal - primal) ** 2) + jnp.sum(capacity_change**2)
         if iteration + 1 < ITERS:
-            primal_total = lax.psum(primal_local, ("tm", "region"))
+            primal_total = lax.psum(lax.psum(primal_local, "tm"), "region")
         applied = network_forward(primal_bar, weights, columns)
         before = shifted(primal_bar[-1, 0], "tm", 1)
         earlier = jnp.concatenate([before[None], primal_bar[:-1, 0]], axis=0)

time: 867 us -> 904 us (1.043)
  blocking collectives: 589 us -> 638 us
  waiting for transfers between devices: 70.8 us -> 59 us
    psum x6 -> x9, blocking collectives: 436 us -> 484 us  [the longest x6 257 us: body(): primal_total = lax.psum(lax.psum(primal_local, 'tm'), 'region')]
    reduce_scatter x4, waiting for transfers between devices: 70.7 us -> 58.9 us  [body(): lax.psum_scatter(jnp.einsum('jq,jhk->qhk', own_sources, partial_lines, pr...]
where the time goes in v1:
time: 904 us; the launch traced here: 895 us
  blocking collectives  638 us (71%)
  matrix products  94.9 us (10%)
  waiting for transfers between devices  59 us (7%)
  other arithmetic  35 us (4%)
  local copies, waits for them, and re-layouts  28.8 us (3%)
  between operations  23.8 us (3%)
  starting transfers between devices  16 us (2%)
    psum x6, blocking collectives, body(): primal_total = lax.psum(lax.psum(primal_local, 'tm'), 'region')  257 us
    psum x3, blocking collectives, body(): dual_total = lax.psum(dual_local, ('tm', 'region'))  228 us
    all_gather x1, blocking collectives, body(): lax.all_gather(start_capacity[0], 'tm', axis=0, tiled=True)  76.9 us
    all_gather x4, blocking collectives, body(): lax.all_gather(primal_bar[:, 3][None], 'region', axis=0, tiled=True)  76.4 us
    reduce_scatter x4, waiting for transfers between devices, body(): lax.psum_scatter(jnp.einsum('jq,jhk->qhk', own_sources, partial_lines, pr...  58.9 us
    dot_general x4, matrix products, network_adjoint(): jnp.einsum('hil,iskl->hisk', dual_rows, weights, precision=HIGHEST_PRECIS...  40.4 us
    dot_general x4, matrix products, network_forward(): jnp.einsum('hpk,pkl->hpl', picked, flat_weights, precision=HIGHEST_PRECIS...  31.7 us
  transfers between devices with their start and end apart: 12, of which 3 were waited for; matrix products, arithmetic and copies ran while one was open for 11% of the time, Pallas kernels for 0%

profile of v1, /device:TPU:1, one launch (start us, length us, event | category | flops | bytes accessed | tf_op | source)
XLA Modules:
  0.0 895.2 jit_solution(10128880783119224581)
XLA Ops:
  12.9 9.0 %fusion.6 = f32[25,64,3,128]{3,1,2,0:T(8,128)S(1)} fusion(f32[1,25,3,128,128]{4,3,2,1,0:T(8,128)} %param.57), kind=kOutput, calls=%fused_computation.10 | convolution fusion | flops 943718400 | bytes 7372800 | tf_op jit(solution)/shard_map/hil,iskl->hisk/dot_general | solution.py:29
  27.1 76.9 %all-reduce.6 = (f32[128]{0:T(128)S(1)}, f32[128]{0:T(128)S(1)}, f32[128]{0:T(128)S(1)}) all-reduce(f32[128]{0:T(128)S(1)} %bitcast_dynamic-update-slice_fusion.1, f32[128]{0:T(128)S(1)} %bitcast_dynamic-update-slice_fusion, f32[128]{0:T(128)S(1)} %fusion.51), channel_id=2, replica_groups=mesh['tm'=32,'region'=8] {'tm'}, use_global_device_ids=true, to_apply=%add.1 | all-reduce | flops 384 | bytes 3072 | tf_op jit(solution)/shard_map/all_gather | solution.py:75
  113.4 28.2 %all-gather.2 = f32[512,1,128]{2,1,0:T(1,128)S(1)} all-gather(f32[64,1,128]{2,1,0:T(1,128)S(1)} %bitcast.385), channel_id=4, replica_groups=mesh['tm'=32,'region'=8] {'region'}, dimensions={0}, use_global_device_ids=true | all-gather | bytes 294912 | tf_op jit(solution)/shard_map/all_gather | solution.py:114
  143.7 7.9 fusion.22
  157.1 10.5 %fusion.4 = f32[25,64,3,128]{3,1,2,0:T(8,128)} fusion(f32[1,25,3,128,128]{4,3,2,1,0:T(8,128)} %param.57, f32[64,25,128]{2,0,1:T(8,128)S(1)} %get-tuple-element.281), kind=kOutput, calls=%fused_computation.8 | convolution fusion | flops 943718400 | bytes 8192000 | tf_op jit(solution)/shard_map/hil,iskl->hisk/dot_general | solution.py:29
  167.6 75.8 %psum.94 = f32[]{:T(128)} all-reduce(f32[]{:T(128)} %get-tuple-element.280), channel_id=1, replica_groups=mesh['tm'=32,'region'=8] {'tm','region'}, use_global_device_ids=true, to_apply=%region_8.10 | all-reduce | flops 1 | bytes 8 | tf_op jit(solution)/shard_map/psum | solution.py:131
  244.3 57.9 %all-reduce.5 = (f32[]{:T(128)}, f32[128]{0:T(128)S(1)}) all-reduce(f32[]{:T(128)S(6)} %add.255, f32[128]{0:T(128)S(1)} %fusion.49), channel_id=1, replica_groups=mesh['tm'=32,'region'=8] {'tm'}, use_global_device_ids=true, to_apply=%region_4.5 | all-reduce | flops 129 | bytes 1032 | tf_op jit(solution)/shard_map/psum | solution.py:107
  302.2 26.7 %psum.93 = f32[]{:T(128)} all-reduce(f32[]{:T(128)} %get-tuple-element.263), channel_id=1, replica_groups=mesh['tm'=32,'region'=8] {'region'}, use_global_device_ids=true, to_apply=%region_5.6 | all-reduce | flops 1 | bytes 8 | tf_op jit(solution)/shard_map/psum | solution.py:107
  340.9 19.9 %reduce-scatter.7.cloned.1.call-done = f32[1,64,128]{2,1,0:T(8,128)} async-done(((f32[8,64,128]{2,1,0:T(8,128)}), f32[1,64,128]{2,1,0:T(8,128)}) %reduce-scatter.7.cloned.1.call-update) | async-done | bytes 32784 | tf_op jit(solution)/shard_map/reduce_scatter | solution.py:87
  370.2 16.1 %all-gather.3 = f32[512,1,128]{2,1,0:T(1,128)S(1)} all-gather(f32[64,1,128]{2,1,0:T(1,128)S(1)} %bitcast.383), channel_id=5, replica_groups=mesh['tm'=32,'region'=8] {'region'}, dimensions={0}, use_global_device_ids=true | all-gather | bytes 294912 | tf_op jit(solution)/shard_map/all_gather | solution.py:114
  386.3 7.9 fusion.20
  399.6 10.5 %fusion.2 = f32[25,64,3,128]{3,1,2,0:T(8,128)} fusion(f32[1,25,3,128,128]{4,3,2,1,0:T(8,128)} %param.57, f32[64,25,128]{2,0,1:T(8,128)S(1)} %get-tuple-element.275), kind=kOutput, calls=%fused_computation.6 | convolution fusion | flops 943718400 | bytes 8192000 | tf_op jit(solution)/shard_map/hil,iskl->hisk/dot_general | solution.py:29
  410.1 76.0 %psum.98 = f32[]{:T(128)} all-reduce(f32[]{:T(128)} %get-tuple-element.274), channel_id=1, replica_groups=mesh['tm'=32,'region'=8] {'tm','region'}, use_global_device_ids=true, to_apply=%region_18.20 | all-reduce | flops 1 | bytes 8 | tf_op jit(solution)/shard_map/psum | solution.py:131
  487.1 58.7 %all-reduce.4 = (f32[]{:T(128)}, f32[128]{0:T(128)S(1)}) all-reduce(f32[]{:T(128)S(6)} %add.263, f32[128]{0:T(128)S(1)} %fusion.47), channel_id=1, replica_groups=mesh['tm'=32,'region'=8] {'tm'}, use_global_device_ids=true, to_apply=%region_14.16 | all-reduce | flops 129 | bytes 1032 | tf_op jit(solution)/shard_map/psum | solution.py:107
  545.8 27.2 %psum.97 = f32[]{:T(128)} all-reduce(f32[]{:T(128)} %get-tuple-element.261), channel_id=1, replica_groups=mesh['tm'=32,'region'=8] {'region'}, use_global_device_ids=true, to_apply=%region_15.17 | all-reduce | flops 1 | bytes 8 | tf_op jit(solution)/shard_map/psum | solution.py:107
  584.7 19.3 %reduce-scatter.9.cloned.1.call-done = f32[1,64,128]{2,1,0:T(8,128)} async-done(((f32[8,64,128]{2,1,0:T(8,128)}), f32[1,64,128]{2,1,0:T(8,128)}) %reduce-scatter.9.cloned.1.call-update) | async-done | bytes 32784 | tf_op jit(solution)/shard_map/reduce_scatter | solution.py:87
  612.6 16.1 %all-gather.4 = f32[512,1,128]{2,1,0:T(1,128)S(1)} all-gather(f32[64,1,128]{2,1,0:T(1,128)S(1)} %bitcast.384), channel_id=6, replica_groups=mesh['tm'=32,'region'=8] {'region'}, dimensions={0}, use_global_device_ids=true | all-gather | bytes 294912 | tf_op jit(solution)/shard_map/all_gather | solution.py:114
  643.3 10.5 %fusion = f32[25,64,3,128]{3,1,2,0:T(8,128)} fusion(f32[1,25,3,128,128]{4,3,2,1,0:T(8,128)} %param.57, f32[64,25,128]{2,0,1:T(8,128)S(1)} %get-tuple-element.271), kind=kOutput, calls=%fused_computation.4 | convolution fusion | flops 943718400 | bytes 8192000 | tf_op jit(solution)/shard_map/hil,iskl->hisk/dot_general | solution.py:29
  653.7 76.0 %psum.102 = f32[]{:T(128)} all-reduce(f32[]{:T(128)} %get-tuple-element.270), channel_id=1, replica_groups=mesh['tm'=32,'region'=8] {'tm','region'}, use_global_device_ids=true, to_apply=%region_28.30 | all-reduce | flops 1 | bytes 8 | tf_op jit(solution)/shard_map/psum | solution.py:131
  730.7 58.7 %all-reduce.3 = (f32[]{:T(128)}, f32[128]{0:T(128)S(1)}) all-reduce(f32[]{:T(128)S(6)} %add.272, f32[128]{0:T(128)S(1)} %fusion.45), channel_id=1, replica_groups=mesh['tm'=32,'region'=8] {'tm'}, use_global_device_ids=true, to_apply=%region_24.26 | all-reduce | flops 129 | bytes 1032 | tf_op jit(solution)/shard_map/psum | solution.py:107
  789.3 27.2 %psum.101 = f32[]{:T(128)} all-reduce(f32[]{:T(128)} %get-tuple-element.259), channel_id=1, replica_groups=mesh['tm'=32,'region'=8] {'region'}, use_global_device_ids=true, to_apply=%region_25.27 | all-reduce | flops 1 | bytes 8 | tf_op jit(solution)/shard_map/psum | solution.py:107
  828.2 19.6 %reduce-scatter.11.cloned.1.call-done = f32[1,64,128]{2,1,0:T(8,128)} async-done(((f32[8,64,128]{2,1,0:T(8,128)}), f32[1,64,128]{2,1,0:T(8,128)}) %reduce-scatter.11.cloned.1.call-update) | async-done | bytes 32784 | tf_op jit(solution)/shard_map/reduce_scatter | solution.py:87
  856.8 16.1 %all-gather.5 = f32[512,1,128]{2,1,0:T(1,128)S(1)} all-gather(f32[64,1,128]{2,1,0:T(1,128)S(1)} %bitcast.382), channel_id=7, replica_groups=mesh['tm'=32,'region'=8] {'region'}, dimensions={0}, use_global_device_ids=true | all-gather | bytes 294912 | tf_op jit(solution)/shard_map/all_gather | solution.py:114
  872.9 8.0 fusion.16
  (185 shorter events, 110.7 us)
Async XLA Ops:
  7.2 97.2 %copy-start = (f32[64,1,3200]{2,1,0:T(1,128)S(1)}, f32[64,1,3200]{2,1,0:T(1,128)}, u32[]{:S(2)}) copy-start(f32[64,1,3200]{2,1,0:T(1,128)} %param.53) | copy-start | bytes 2457604
  7.2 103.0 %reduce-scatter.5.cloned.1.call-start = ((), (), s32[]{:S(2)}) async-start(), calls=%async_computation.4 | async-start | bytes 294912 | tf_op jit(solution)/shard_map/reduce_scatter | solution.py:87
  7.2 102.9 %collective-permute-start = (f32[128]{0:T(128)S(1)}, f32[128]{0:T(128)S(1)}, u32[]{:S(2)}, u32[]{:S(2)}) collective-permute-start(f32[128]{0:T(128)S(1)} %broadcast.305), channel_id=1, source_target_pairs={{8,0},{16,8},{24,16},{32,24},{40,32},{48,40},{56,48},{64,56},{72,6... | collective-permute-start | bytes 1544 | tf_op jit(solution)/shard_map/ppermute | solution.py:16
  12.0 348.8 %reduce-scatter.7.cloned.1.call-start = ((), (), s32[]{:S(2)}) async-start(), calls=%async_computation.5 | async-start | bytes 294912 | tf_op jit(solution)/shard_map/reduce_scatter | solution.py:87
  24.4 2.6 copy-start.13
  24.4 79.8 %copy-start.11 = (f32[1,3200]{1,0:T(1,128)S(1)}, f32[1,3200]{1,0:T(1,128)}, u32[]{:S(2)}) copy-start(f32[1,3200]{1,0:T(1,128)} %param.54) | copy-start | bytes 38404
  112.1 43.3 %collective-permute-start.1 = (f32[128]{0:T(128)S(1)}, f32[128]{0:T(128)S(1)}, u32[]{:S(2)}, u32[]{:S(2)}) collective-permute-start(f32[128]{0:T(128)S(1)} %slice_bitcast_fusion.16), channel_id=1, source_target_pairs={{0,8},{8,16},{16,24},{24,32},{32,40},{40,48},{48,56},{56,64},{64,7... | collective-permute-start | bytes 1544 | tf_op jit(solution)/shard_map/ppermute | solution.py:16
  151.6 3.8 copy-start.2
  156.7 10.9 %copy-start.8 = (f32[64,25,128]{2,0,1:T(8,128)}, f32[64,25,128]{2,0,1:T(8,128)S(1)}, u32[]{:S(2)}) copy-start(f32[64,25,128]{2,0,1:T(8,128)S(1)} %get-tuple-element.281) | copy-start | bytes 2457604
  243.6 93.2 %copy-start.15 = (s32[1,128]{1,0:T(1,128)S(1)}, s32[1,128]{1,0:T(1,128)}, u32[]{:S(2)}) copy-start(s32[1,128]{1,0:T(1,128)} %param.61) | copy-start | bytes 1540
  329.7 10.5 %collective-permute-start.2 = (f32[128]{0:T(128)S(1)}, f32[128]{0:T(128)S(1)}, u32[]{:S(2)}, u32[]{:S(2)}) collective-permute-start(f32[128]{0:T(128)S(1)} %slice_bitcast_fusion.15), channel_id=1, source_target_pairs={{8,0},{16,8},{24,16},{32,24},{40,32},{48,40},{56,48},{64,56},{72,6... | collective-permute-start | bytes 1544 | tf_op jit(solution)/shard_map/ppermute | solution.py:16
  332.2 271.9 %reduce-scatter.9.cloned.1.call-start = ((), (), s32[]{:S(2)}) async-start(), calls=%async_computation.6 | async-start | bytes 294912 | tf_op jit(solution)/shard_map/reduce_scatter | solution.py:87
  367.4 30.5 %collective-permute-start.3 = (f32[128]{0:T(128)S(1)}, f32[128]{0:T(128)S(1)}, u32[]{:S(2)}, u32[]{:S(2)}) collective-permute-start(f32[128]{0:T(128)S(1)} %slice_bitcast_fusion.14), channel_id=1, source_target_pairs={{0,8},{8,16},{16,24},{24,32},{32,40},{40,48},{48,56},{56,64},{64,7... | collective-permute-start | bytes 1544 | tf_op jit(solution)/shard_map/ppermute | solution.py:16
  394.2 4.0 copy-start.9
  399.2 10.9 %copy-start.7 = (f32[64,25,128]{2,0,1:T(8,128)}, f32[64,25,128]{2,0,1:T(8,128)S(1)}, u32[]{:S(2)}) copy-start(f32[64,25,128]{2,0,1:T(8,128)S(1)} %get-tuple-element.275) | copy-start | bytes 2457604
  573.8 10.3 %collective-permute-start.4 = (f32[128]{0:T(128)S(1)}, f32[128]{0:T(128)S(1)}, u32[]{:S(2)}, u32[]{:S(2)}) collective-permute-start(f32[128]{0:T(128)S(1)} %slice_bitcast_fusion.13), channel_id=1, source_target_pairs={{8,0},{16,8},{24,16},{32,24},{40,32},{48,40},{56,48},{64,56},{72,6... | collective-permute-start | bytes 1544 | tf_op jit(solution)/shard_map/ppermute | solution.py:16
  576.3 271.5 %reduce-scatter.11.cloned.1.call-start = ((), (), s32[]{:S(2)}) async-start(), calls=%async_computation.7 | async-start | bytes 294912 | tf_op jit(solution)/shard_map/reduce_scatter | solution.py:87
  580.5 24.9 %copy-start.4 = (f32[64,25,128]{2,0,1:T(8,128)S(1)}, f32[64,25,128]{2,0,1:T(8,128)}, u32[]{:S(2)}) copy-start(f32[64,25,128]{2,0,1:T(8,128)} %copy-done.3) | copy-start | bytes 2457604
  609.8 30.5 %collective-permute-start.5 = (f32[128]{0:T(128)S(1)}, f32[128]{0:T(128)S(1)}, u32[]{:S(2)}, u32[]{:S(2)}) collective-permute-start(f32[128]{0:T(128)S(1)} %slice_bitcast_fusion.12), channel_id=1, source_target_pairs={{0,8},{8,16},{16,24},{24,32},{32,40},{40,48},{48,56},{56,64},{64,7... | collective-permute-start | bytes 1544 | tf_op jit(solution)/shard_map/ppermute | solution.py:16
  642.8 10.9 %copy-start.5 = (f32[64,25,128]{2,0,1:T(8,128)}, f32[64,25,128]{2,0,1:T(8,128)S(1)}, u32[]{:S(2)}) copy-start(f32[64,25,128]{2,0,1:T(8,128)S(1)} %get-tuple-element.271) | copy-start | bytes 2457604
  817.4 10.2 %collective-permute-start.6 = (f32[128]{0:T(128)S(1)}, f32[128]{0:T(128)S(1)}, u32[]{:S(2)}, u32[]{:S(2)}) collective-permute-start(f32[128]{0:T(128)S(1)} %slice_bitcast_fusion.11), channel_id=1, source_target_pairs={{8,0},{16,8},{24,16},{32,24},{40,32},{48,40},{56,48},{64,56},{72,6... | collective-permute-start | bytes 1544 | tf_op jit(solution)/shard_map/ppermute | solution.py:16
  854.0 31.6 %collective-permute-start.7 = (f32[128]{0:T(128)S(1)}, f32[128]{0:T(128)S(1)}, u32[]{:S(2)}, u32[]{:S(2)}) collective-permute-start(f32[128]{0:T(128)S(1)} %slice_bitcast_fusion.10), channel_id=1, source_target_pairs={{0,8},{8,16},{16,24},{24,32},{32,40},{40,48},{48,56},{56,64},{64,7... | collective-permute-start | bytes 1544 | tf_op jit(solution)/shard_map/ppermute | solution.py:16
  872.9 8.4 copy-start.10
  881.8 4.1 copy-start.6
  (5 other events, 8.1 us)
Sparse Core Ops, SparseCore 0:
  12.1 36.2 reduce-scatter.4
  332.3 28.4 reduce-scatter.6
  576.4 27.6 reduce-scatter.8
  820.2 27.5 reduce-scatter.10
